TPU v7x, 512 devices: a whole 4x8x8 slice. The times are simulated.
512 devices in a mesh: tick: 64 (over y, z_hi, core), wire: 8 (over z_lo, x).
Axes of the slice: x: 4, y: 8, z: 8 (z_hi: 4, z_lo: 2; z = z_hi * 2 + z_lo), core: 2. Of those that a mesh axis runs over, the one named last changes fastest.
Arguments:
- signal: float32 [16, 512, 8192], P(None, 'wire', 'tick'), may hold values from -6 to 6
- kernel_front: float32 [16, 3, 9], replicated, may hold values from -1.25 to 1.25
- mixing_front: float32 [16, 16], replicated, may hold values from -1.5 to 1.5
- offset_front: float32 [16], replicated, may hold values from -2 to 2
- kernel_back: float32 [16, 3, 9], replicated, may hold values from -1.25 to 1.25
- mixing_back: float32 [16, 16], replicated, may hold values from -1.5 to 1.5
- offset_back: float32 [16], replicated, may hold values from -2 to 2
- upstream: float32 [16, 512, 8192], P(None, 'wire', 'tick'), may hold values from -13 to 13
Outputs:
- response: float32 [16, 512, 8192], P(None, 'wire', 'tick')
- signal_grad: float32 [16, 512, 8192], P(None, 'wire', 'tick')
- kernel_front_grad: float32 [16, 3, 9], replicated
- mixing_front_grad: float32 [16, 16], replicated
- offset_front_grad: float32 [16], replicated
- kernel_back_grad: float32 [16, 3, 9], replicated
- mixing_back_grad: float32 [16, 16], replicated
- offset_back_grad: float32 [16], replicated
All inputs are finite; a program needn't handle non-finite values.
Results may differ from a plain program's by a relative error of at most 0.0003.
Values sent between devices are 32-bit elements; how exact they have to be, the bound alone decides.
No kernel may reach another device: no remote copies, remote signals or barrier semaphores. Data moves between devices by JAX's collectives and lax.ppermute only.
A program may use at most 64 MiB of HBM per device.

v0:
```python
import math
import jax
import jax.numpy as jnp
from jax import lax
from jax.sharding import PartitionSpec as P

TICK_DILATION = 8


def with_halo(block, sides, width):
    for axis, dim in sides:
        count = lax.axis_size(axis)
        forward = [(i, i + 1) for i in range(count - 1)]
        backward = [(target, source) for source, target in forward]
        low = lax.ppermute(
            lax.slice_in_dim(block, block.shape[dim] - width, None, axis=dim), axis, forward
        )
        high = lax.ppermute(lax.slice_in_dim(block, 0, width, axis=dim), axis, backward)
        block = jnp.concatenate([low, block, high], axis=dim)
    return block


def spread(field, tick_deep, wire_deep):
    longer = with_halo(field, (("tick", 2),), tick_deep)
    return with_halo(longer, (("wire", 1),), wire_deep)


def depthwise(padded_input, kernel_weight, row_count, column_count):
    total_sum = jnp.zeros((padded_input.shape[0], row_count, column_count), jnp.float32)
    for row_index in range(3):
        for column_index in range(9):
            total_sum = (
                total_sum
                + kernel_weight[:, row_index, column_index][:, None, None]
                * padded_input[
                    :,
                    row_index : row_index + row_count,
                    TICK_DILATION * column_index : TICK_DILATION * column_index + column_count,
                ]
            )
    return total_sum


def tap_grads(upward_gradient, padded_input):
    row_count = upward_gradient.shape[1]
    column_count = upward_gradient.shape[2]
    text_lines = []
    for row_index in range(3):
        text_lines.append(
            jnp.stack(
                [
                    jnp.sum(
                        upward_gradient
                        * padded_input[
                            :,
                            row_index : row_index + row_count,
                            TICK_DILATION * column_index : TICK_DILATION * column_index
                            + column_count,
                        ],
                        axis=(1, 2),
                    )
                    for column_index in range(9)
                ],
                axis=1,
            )
        )
    return jnp.stack(text_lines, axis=1)


def mixing(matrix, field, offset):
    return (
        jnp.einsum("oc,cwt->owt", matrix, field, precision=lax.Precision.HIGHEST)
        + offset[:, None, None]
    )


def slope(preact):
    sig = jax.nn.sigmoid(preact)
    return sig * (1.0 + preact * (1.0 - sig))


def per_device(
    signal,
    kernel_front,
    mixing_front,
    offset_front,
    kernel_back,
    mixing_back,
    offset_back,
    upstream,
):
    row_count = signal.shape[1]
    column_count = signal.shape[2]
    kernel_extent = 4 * TICK_DILATION
    padded_in = spread(signal, kernel_extent, 1)
    taps_front = depthwise(padded_in, kernel_front, row_count, column_count)
    pre_front = mixing(mixing_front, taps_front, offset_front)
    padded_act = spread(jax.nn.silu(pre_front), kernel_extent, 1)
    taps_back = depthwise(padded_act, kernel_back, row_count, column_count)
    pre_back = mixing(mixing_back, taps_back, offset_back)
    response = jax.nn.silu(pre_back)
    grad_back = upstream * slope(pre_back)
    gmix_back = jnp.einsum("owt,cwt->oc", grad_back, taps_back, precision=lax.Precision.HIGHEST)
    gbias_back = jnp.sum(grad_back, axis=(1, 2))
    under_back = jnp.einsum("oc,owt->cwt", mixing_back, grad_back, precision=lax.Precision.HIGHEST)
    gkern_back = tap_grads(under_back, padded_act)
    into_front = depthwise(
        spread(under_back, kernel_extent, 1), kernel_back[:, ::-1, ::-1], row_count, column_count
    )
    grad_front = into_front * slope(pre_front)
    gmix_front = jnp.einsum("owt,cwt->oc", grad_front, taps_front, precision=lax.Precision.HIGHEST)
    gbias_front = jnp.sum(grad_front, axis=(1, 2))
    under_front = jnp.einsum(
        "oc,owt->cwt", mixing_front, grad_front, precision=lax.Precision.HIGHEST
    )
    gkern_front = tap_grads(under_front, padded_in)
    signal_grad = depthwise(
        spread(under_front, kernel_extent, 1), kernel_front[:, ::-1, ::-1], row_count, column_count
    )
    totals = lax.psum(
        (gkern_front, gmix_front, gbias_front, gkern_back, gmix_back, gbias_back), ("tick", "wire")
    )
    factor = 1.0 / math.sqrt(
        row_count * lax.axis_size("wire") * column_count * lax.axis_size("tick")
    )
    return (
        response,
        signal_grad,
        totals[0] * factor,
        totals[1] * factor,
        totals[2] * factor,
        totals[3] * factor,
        totals[4] * factor,
        totals[5] * factor,
    )


def solution(mesh):
    in_specs = (P(None, "wire", "tick"), P(), P(), P(), P(), P(), P(), P(None, "wire", "tick"))
    out_specs = (P(None, "wire", "tick"), P(None, "wire", "tick"), P(), P(), P(), P(), P(), P())
    return jax.shard_map(
        per_device, mesh=mesh, in_specs=in_specs, out_specs=out_specs, check_vma=False
    )
```

profile of v0, /device:TPU:30, one launch (start us, length us, event | category | flops | bytes accessed | tf_op | source)
XLA Modules:
  0.0 259.0 jit_solution(9432671093252713411)
XLA Ops:
  0.6 0.0 copy-start
  0.6 1.4 constant_dynamic-update-slice_fusion.1
  2.0 0.0 copy-start.15
  2.0 0.2 fusion.104
  2.2 1.9 collective-permute-start
  4.1 10.3 %collective-permute-start.1 = (f32[16,64,32]{2,0,1:T(8,128)S(1)}, f32[16,64,32]{2,0,1:T(8,128)S(1)}, u32[]{:S(2)}, u32[]{:S(2)}) collective-permute-start(f32[16,64,32]{2,0,1:T(8,128)S(1)} %get-tuple-element.132), channel_id=1, source_target_pairs={{8,0},{16,8},{24,16},{32,24},{40,32},{48,40},{56,48},{64,56},{72,6... | collective-permute-start | bytes 393224 | tf_op jit(solution)/shard_map/ppermute | solution.py:18
  14.5 9.6 %collective-permute-done = f32[16,64,32]{2,0,1:T(8,128)S(1)} collective-permute-done((f32[16,64,32]{2,0,1:T(8,128)S(1)}, f32[16,64,32]{2,0,1:T(8,128)S(1)}, u32[]{:S(2)}, u32[]{:S(2)}) %collective-permute-start) | collective-permute-done | bytes 131104 | tf_op jit(solution)/shard_map/ppermute | solution.py:15
  24.0 1.3 collective-permute-done.1
  25.3 0.1 pad_maximum_fusion.24
  25.4 2.9 %collective-permute-start.2 = (f32[16,1,192]{2,0,1:T(8,128)S(1)}, f32[16,1,192]{2,0,1:T(8,128)S(1)}, u32[]{:S(2)}, u32[]{:S(2)}) collective-permute-start(f32[16,1,192]{2,0,1:T(8,128)S(1)} %get-tuple-element.120), channel_id=1, source_target_pairs={{0,1},{1,2},{2,3},{3,4},{4,5},{5,6},{6,7},{8,9},{9,10},{10,11},{11... | collective-permute-start | bytes 36872 | tf_op jit(solution)/shard_map/ppermute | solution.py:15
  28.3 2.9 %collective-permute-start.3 = (f32[16,1,192]{2,0,1:T(8,128)S(1)}, f32[16,1,192]{2,0,1:T(8,128)S(1)}, u32[]{:S(2)}, u32[]{:S(2)}) collective-permute-start(f32[16,1,192]{2,0,1:T(8,128)S(1)} %get-tuple-element.121), channel_id=1, source_target_pairs={{1,0},{2,1},{3,2},{4,3},{5,4},{6,5},{7,6},{9,8},{10,9},{11,10},{12... | collective-permute-start | bytes 36872 | tf_op jit(solution)/shard_map/ppermute | solution.py:18
  31.3 0.1 constant_dynamic-update-slice_fusion
  31.3 4.7 %collective-permute-done.3 = f32[16,1,192]{2,0,1:T(8,128)S(1)} collective-permute-done((f32[16,1,192]{2,0,1:T(8,128)S(1)}, f32[16,1,192]{2,0,1:T(8,128)S(1)}, u32[]{:S(2)}, u32[]{:S(2)}) %collective-permute-start.3) | collective-permute-done | bytes 12320 | tf_op jit(solution)/shard_map/ppermute | solution.py:18
  36.1 0.9 maximum_maximum_fusion
  37.0 0.0 copy-start.18
  37.0 0.0 copy-start.19
  37.0 3.9 %multiply_add_fusion.1 = f32[16,64,128]{2,0,1:T(8,128)S(1)} fusion(f32[16,64,128]{2,0,1:T(8,128)S(1)} %get-tuple-element.130, f32[16,65,192]{2,0,1:T(8,128)S(1)} %get-tuple-element.119, f32[16,64,160]{2,0,1:T(8,128)S(1)} %constant_dynamic-update-slice_fusion, f32[16,65,192]{2,0,1:T(8,128)S(1)} %get-tuple-element.118, f32[16]{0:T(128)S(1)} %get-tuple-element.185, ...), kind=kLoop, calls=%fused_computation.251 | loop fusion | flops 7471104 | bytes 12715712 | tf_op jit(solution)/shard_map/add | solution.py:33
  41.0 1.4 fusion.93
  42.4 0.2 fusion.103
  42.6 2.4 collective-permute-start.4
  45.1 6.1 %collective-permute-start.5 = (f32[16,64,32]{2,0,1:T(8,128)S(1)}, f32[16,64,32]{2,0,1:T(8,128)S(1)}, u32[]{:S(2)}, u32[]{:S(2)}) collective-permute-start(f32[16,64,32]{2,0,1:T(8,128)S(1)} %get-tuple-element.128), channel_id=1, source_target_pairs={{8,0},{16,8},{24,16},{32,24},{40,32},{48,40},{56,48},{64,56},{72,6... | collective-permute-start | bytes 393224 | tf_op jit(solution)/shard_map/ppermute | solution.py:18
  51.2 7.9 %collective-permute-done.4 = f32[16,64,32]{2,0,1:T(8,128)S(1)} collective-permute-done((f32[16,64,32]{2,0,1:T(8,128)S(1)}, f32[16,64,32]{2,0,1:T(8,128)S(1)}, u32[]{:S(2)}, u32[]{:S(2)}) %collective-permute-start.4) | collective-permute-done | bytes 131104 | tf_op jit(solution)/shard_map/ppermute | solution.py:15
  59.1 1.6 collective-permute-done.5
  60.7 0.1 pad_maximum_fusion.21
  60.7 2.7 %collective-permute-start.6 = (f32[16,1,192]{2,0,1:T(8,128)S(1)}, f32[16,1,192]{2,0,1:T(8,128)S(1)}, u32[]{:S(2)}, u32[]{:S(2)}) collective-permute-start(f32[16,1,192]{2,0,1:T(8,128)S(1)} %get-tuple-element.116), channel_id=1, source_target_pairs={{0,1},{1,2},{2,3},{3,4},{4,5},{5,6},{6,7},{8,9},{9,10},{10,11},{11... | collective-permute-start | bytes 36872 | tf_op jit(solution)/shard_map/ppermute | solution.py:15
  63.5 3.1 %collective-permute-start.7 = (f32[16,1,192]{2,0,1:T(8,128)S(1)}, f32[16,1,192]{2,0,1:T(8,128)S(1)}, u32[]{:S(2)}, u32[]{:S(2)}) collective-permute-start(f32[16,1,192]{2,0,1:T(8,128)S(1)} %get-tuple-element.117), channel_id=1, source_target_pairs={{1,0},{2,1},{3,2},{4,3},{5,4},{6,5},{7,6},{9,8},{10,9},{11,10},{12... | collective-permute-start | bytes 36872 | tf_op jit(solution)/shard_map/ppermute | solution.py:18
  66.6 4.6 %collective-permute-done.7 = f32[16,1,192]{2,0,1:T(8,128)S(1)} collective-permute-done((f32[16,1,192]{2,0,1:T(8,128)S(1)}, f32[16,1,192]{2,0,1:T(8,128)S(1)}, u32[]{:S(2)}, u32[]{:S(2)}) %collective-permute-start.7) | collective-permute-done | bytes 12320 | tf_op jit(solution)/shard_map/ppermute | solution.py:18
  71.2 0.9 maximum_maximum_fusion.1
  72.1 0.0 copy-start.17
  72.1 0.0 copy-start.20
  72.1 4.5 %multiply_add_fusion = f32[16,64,128]{2,0,1:T(8,128)S(1)} fusion(f32[16,64,128]{2,0,1:T(8,128)S(1)} %get-tuple-element.187, f32[16,65,192]{2,0,1:T(8,128)S(1)} %get-tuple-element.115, f32[16,65,192]{2,0,1:T(8,128)S(1)} %get-tuple-element.114, f32[16]{0:T(128)S(1)} %get-tuple-element.158, f32[16]{0:T(128)S(1)} %get-tuple-element.159, ...), kind=kLoop, calls=%fused_computation.248 | loop fusion | flops 7995392 | bytes 10749632 | tf_op jit(solution)/shard_map/add | solution.py:33
  76.7 1.8 fusion.98
  78.5 3.0 %multiply_reduce_fusion.18 = (f32[16]{0:T(128)S(1)}, f32[16]{0:T(128)S(1)}, f32[16]{0:T(128)S(1)}, f32[16]{0:T(128)S(1)}, f32[16]{0:T(128)S(1)}, /*index=5*/f32[...) fusion(f32[16,65,192]{2,0,1:T(8,128)S(1)} %get-tuple-element.11, ...), kind=kOutput, calls=%fused_computation.210 | convolution fusion | flops 29884128 | bytes 10487936 | tf_op jit(solution)/shard_map/oc,owt->cwt/dot_general | solution.py:105
  81.5 1.1 fusion.102
  82.7 4.1 %collective-permute-start.8 = (f32[16,64,32]{2,0,1:T(8,128)}, f32[16,64,32]{2,0,1:T(8,128)}, u32[]{:S(2)}, u32[]{:S(2)}) collective-permute-start(f32[16,64,32]{2,0,1:T(8,128)} %get-tuple-element.124), channel_id=1, source_target_pairs={{0,8},{8,16},{16,24},{24,32},{32,40},{40,48},{48,56},{56,64},{64,7... | collective-permute-start | bytes 393224 | tf_op jit(solution)/shard_map/ppermute | solution.py:15
  86.8 4.7 %collective-permute-start.9 = (f32[16,64,32]{2,0,1:T(8,128)}, f32[16,64,32]{2,0,1:T(8,128)}, u32[]{:S(2)}, u32[]{:S(2)}) collective-permute-start(f32[16,64,32]{2,0,1:T(8,128)} %get-tuple-element.125), channel_id=1, source_target_pairs={{8,0},{16,8},{24,16},{32,24},{40,32},{48,40},{56,48},{64,56},{72,6... | collective-permute-start | bytes 393224 | tf_op jit(solution)/shard_map/ppermute | solution.py:18
  91.5 4.9 %multiply_reduce_fusion.9 = (f32[16]{0:T(128)S(1)}, f32[16]{0:T(128)S(1)}, f32[16]{0:T(128)S(1)}, f32[16]{0:T(128)S(1)}, f32[16]{0:T(128)S(1)}, /*index=5*/f32[1...) fusion(f32[16,64,128]{2,0,1:T(8,128)} %copy-done.3, f32[16,64,32]{2,0,1:T(8,128)} %copy-done.8, ...), kind=kLoop, calls=%fused_computation.201 | loop fusion | flops 3932016 | bytes 1835584 | tf_op jit(solution)/shard_map/reduce_sum | solution.py:52
  96.5 2.0 convolution_bitcast_fusion.2
  98.5 1.1 collective-permute-done.9
  99.6 0.8 pad_maximum_fusion.18
  100.4 4.2 %collective-permute-start.10 = (f32[16,1,192]{2,0,1:T(8,128)S(1)}, f32[16,1,192]{2,0,1:T(8,128)S(1)}, u32[]{:S(2)}, u32[]{:S(2)}) collective-permute-start(f32[16,1,192]{2,0,1:T(8,128)S(1)} %get-tuple-element.112), channel_id=1, source_target_pairs={{0,1},{1,2},{2,3},{3,4},{4,5},{5,6},{6,7},{8,9},{9,10},{10,11},{11... | collective-permute-start | bytes 36872 | tf_op jit(solution)/shard_map/ppermute | solution.py:15
  104.6 1.9 collective-permute-start.11
  106.5 1.0 copy.26
  107.5 4.8 %collective-permute-done.11 = f32[16,1,192]{2,0,1:T(8,128)S(1)} collective-permute-done((f32[16,1,192]{2,0,1:T(8,128)S(1)}, f32[16,1,192]{2,0,1:T(8,128)S(1)}, u32[]{:S(2)}, u32[]{:S(2)}) %collective-permute-start.11) | collective-permute-done | bytes 12320 | tf_op jit(solution)/shard_map/ppermute | solution.py:18
  112.3 2.4 maximum_maximum_fusion.2
  114.8 6.4 %fusion.99 = (f32[16]{0:T(128)S(1)}, f32[16,64,128]{2,0,1:T(8,128)S(1)}) fusion(f32[16,64,128]{2,0,1:T(8,128)S(1)} %copy-done.12, f32[16,65,192]{2,0,1:T(8,128)S(1)} %get-tuple-element.111, f32[16]{0:T(128)S(1)} %get-tuple-element.133, f32[16]{0:T(128)S(1)} %get-tuple-element.152, f32[16]{0:T(128)S(1)} %get-tuple-element.157, f32[16]{0:T(128)S(1)} %get-tuple-element.156, ...), kind=kLoop, calls=%fused_computation.333 | loop fusion | flops 9175024 | bytes 11273984 | tf_op jit(solution)/shard_map/reduce_sum | solution.py:112
  121.2 0.8 convolution_bitcast_fusion.3
  122.0 3.0 %multiply_reduce_fusion.45 = (f32[16]{0:T(128)S(1)}, f32[16]{0:T(128)S(1)}, f32[16]{0:T(128)S(1)}, f32[16]{0:T(128)S(1)}, f32[16]{0:T(128)S(1)}, /*index=5*/f32[...) fusion(f32[16,65,192]{2,0,1:T(8,128)S(1)} %get-tuple-element.11, ...), kind=kOutput, calls=%fused_computation.237 | convolution fusion | flops 29884128 | bytes 10487936 | tf_op jit(solution)/shard_map/oc,owt->cwt/dot_general | solution.py:113
  125.1 1.1 fusion.101
  126.2 3.7 %collective-permute-start.12 = (f32[16,64,32]{2,0,1:T(8,128)}, f32[16,64,32]{2,0,1:T(8,128)S(1)}, u32[]{:S(2)}, u32[]{:S(2)}) collective-permute-start(f32[16,64,32]{2,0,1:T(8,128)} %get-tuple-element.122), channel_id=1, source_target_pairs={{0,8},{8,16},{16,24},{24,32},{32,40},{40,48},{48,56},{56,64},{64,7... | collective-permute-start | bytes 393224 | tf_op jit(solution)/shard_map/ppermute | solution.py:15
  129.9 4.8 %collective-permute-start.13 = (f32[16,64,32]{2,0,1:T(8,128)}, f32[16,64,32]{2,0,1:T(8,128)}, u32[]{:S(2)}, u32[]{:S(2)}) collective-permute-start(f32[16,64,32]{2,0,1:T(8,128)} %get-tuple-element.123), channel_id=1, source_target_pairs={{8,0},{16,8},{24,16},{32,24},{40,32},{48,40},{56,48},{64,56},{72,6... | collective-permute-start | bytes 393224 | tf_op jit(solution)/shard_map/ppermute | solution.py:18
  134.8 2.9 %multiply_reduce_fusion.36 = (f32[16]{0:T(128)S(1)}, f32[16]{0:T(128)S(1)}, f32[16]{0:T(128)S(1)}, f32[16]{0:T(128)S(1)}, f32[16]{0:T(128)S(1)}, /*index=5*/f32[...) fusion(f32[16,64,128]{2,0,1:T(8,128)S(1)} %get-tuple-element.189, f32[16,64,160]{2,0,1:T(8,128)S(1)} %copy-done.2, ...), kind=kLoop, calls=%fused_computation.228 | loop fusion | flops 2883440 | bytes 3801664 | tf_op jit(solution)/shard_map/reduce_sum | solution.py:52
  137.8 98.3 %all-reduce = (f32[16,3,9]{0,2,1:T(8,128)S(1)}, f32[16,16]{1,0:T(8,128)S(1)}, f32[16]{0:T(128)S(1)}, f32[16,3,9]{0,2,1:T(8,128)S(1)}, f32[16,16]{1,0:T(8,128)S(1)}, /*index=5*/f32[16]{0:T(128)S(1)}) all-reduce(f32[16,3,9]{0,2,1:T(8,128)S(1)} %pad_maximum_fusion.11, ...), channel_id=1, replica_groups=mesh['tick'=64,'wire'=8] {'tick','wire'}, use_global_device_ids=true, to_apply=%region_27.28 | all-reduce | flops 1408 | bytes 11264 | tf_op jit(solution)/shard_map/psum | solution.py:120
  236.1 0.6 broadcast_multiply_fusion.2
  236.7 0.8 pad_maximum_fusion.15
  237.5 5.0 %collective-permute-start.14 = (f32[16,1,192]{2,0,1:T(8,128)S(1)}, f32[16,1,192]{2,0,1:T(8,128)S(1)}, u32[]{:S(2)}, u32[]{:S(2)}) collective-permute-start(f32[16,1,192]{2,0,1:T(8,128)S(1)} %get-tuple-element.108), channel_id=1, source_target_pairs={{0,1},{1,2},{2,3},{3,4},{4,5},{5,6},{6,7},{8,9},{9,10},{10,11},{11... | collective-permute-start | bytes 36872 | tf_op jit(solution)/shard_map/ppermute | solution.py:15
  242.4 2.1 collective-permute-start.15
  244.6 0.5 broadcast_multiply_fusion.4
  245.1 0.6 copy.28
  245.7 0.6 copy.29
  246.3 3.8 %collective-permute-done.15 = f32[16,1,192]{2,0,1:T(8,128)S(1)} collective-permute-done((f32[16,1,192]{2,0,1:T(8,128)S(1)}, f32[16,1,192]{2,0,1:T(8,128)S(1)}, u32[]{:S(2)}, u32[]{:S(2)}) %collective-permute-start.15) | collective-permute-done | bytes 12320 | tf_op jit(solution)/shard_map/ppermute | solution.py:18
  250.2 2.1 maximum_maximum_fusion.3
  252.3 5.7 %fusion.14 = f32[16,64,128]{2,0,1:T(8,128)S(1)} fusion(f32[16,64,128]{2,0,1:T(8,128)S(1)} %get-tuple-element.189, f32[16,64,32]{2,0,1:T(8,128)} %collective-permute-done.13, f32[16,64,32]{2,0,1:T(8,128)S(1)} %collective-permute-done.12, f32[16,65,192]{2,0,1:T(8,128)S(1)} %get-tuple-element.107, f32[16,65,192]{2,0,1:T(8,128)S(1)} %get-tuple-element.106, ...), kind=kLoop, calls=%fused_computation.70 | loop fusion | flops 7995392 | bytes 10749632 | tf_op jit(solution)/shard_map/add | solution.py:33
  258.0 1.0 copy.27
  (56 shorter events, 0.4 us)
Async XLA Ops:
  0.6 76.0 %copy-start = (f32[16,16]{1,0:T(8,128)S(1)}, f32[16,16]{1,0:T(8,128)}, u32[]{:S(2)}) copy-start(f32[16,16]{1,0:T(8,128)} %param.13) | copy-start | bytes 3076
  2.0 12.4 %copy-start.15 = (f32[16,3,9]{0,1,2:T(4,128)S(1)}, f32[16,3,9]{0,1,2:T(4,128)}, u32[]{:S(2)}) copy-start(f32[16,3,9]{0,1,2:T(4,128)} %param.9) | copy-start | bytes 5188
  2.2 21.8 %collective-permute-start = (f32[16,64,32]{2,0,1:T(8,128)S(1)}, f32[16,64,32]{2,0,1:T(8,128)S(1)}, u32[]{:S(2)}, u32[]{:S(2)}) collective-permute-start(f32[16,64,32]{2,0,1:T(8,128)S(1)} %get-tuple-element.131), channel_id=1, source_target_pairs={{0,8},{8,16},{16,24},{24,32},{32,40},{40,48},{48,56},{56,64},{64,7... | collective-permute-start | bytes 393224 | tf_op jit(solution)/shard_map/ppermute | solution.py:15
  4.1 21.2 %collective-permute-start.1 = (f32[16,64,32]{2,0,1:T(8,128)S(1)}, f32[16,64,32]{2,0,1:T(8,128)S(1)}, u32[]{:S(2)}, u32[]{:S(2)}) collective-permute-start(f32[16,64,32]{2,0,1:T(8,128)S(1)} %get-tuple-element.132), channel_id=1, source_target_pairs={{8,0},{16,8},{24,16},{32,24},{40,32},{48,40},{56,48},{64,56},{72,6... | collective-permute-start | bytes 393224 | tf_op jit(solution)/shard_map/ppermute | solution.py:18
  24.0 12.9 %copy-start.5 = (f32[16,64,32]{2,0,1:T(8,128)}, f32[16,64,32]{2,0,1:T(8,128)S(1)}, u32[]{:S(2)}) copy-start(f32[16,64,32]{2,0,1:T(8,128)S(1)} %collective-permute-done) | copy-start | bytes 393220
  25.4 5.9 %collective-permute-start.2 = (f32[16,1,192]{2,0,1:T(8,128)S(1)}, f32[16,1,192]{2,0,1:T(8,128)S(1)}, u32[]{:S(2)}, u32[]{:S(2)}) collective-permute-start(f32[16,1,192]{2,0,1:T(8,128)S(1)} %get-tuple-element.120), channel_id=1, source_target_pairs={{0,1},{1,2},{2,3},{3,4},{4,5},{5,6},{6,7},{8,9},{9,10},{10,11},{11... | collective-permute-start | bytes 36872 | tf_op jit(solution)/shard_map/ppermute | solution.py:15
  28.3 7.7 %collective-permute-start.3 = (f32[16,1,192]{2,0,1:T(8,128)S(1)}, f32[16,1,192]{2,0,1:T(8,128)S(1)}, u32[]{:S(2)}, u32[]{:S(2)}) collective-permute-start(f32[16,1,192]{2,0,1:T(8,128)S(1)} %get-tuple-element.121), channel_id=1, source_target_pairs={{1,0},{2,1},{3,2},{4,3},{5,4},{6,5},{7,6},{9,8},{10,9},{11,10},{12... | collective-permute-start | bytes 36872 | tf_op jit(solution)/shard_map/ppermute | solution.py:18
  31.3 5.7 %copy-start.1 = (f32[16,64,160]{2,0,1:T(8,128)}, f32[16,64,160]{2,0,1:T(8,128)S(1)}, u32[]{:S(2)}) copy-start(f32[16,64,160]{2,0,1:T(8,128)S(1)} %constant_dynamic-update-slice_fusion) | copy-start | bytes 1966084
  37.0 4.0 %copy-start.18 = (f32[16,16]{1,0:T(8,128)S(1)}, f32[16,16]{1,0:T(8,128)}, u32[]{:S(2)}) copy-start(f32[16,16]{1,0:T(8,128)} %param.10) | copy-start | bytes 3076
  37.0 4.0 %copy-start.19 = (f32[16]{0:T(128)S(1)}, f32[16]{0:T(128)}, u32[]{:S(2)}) copy-start(f32[16]{0:T(128)} %param.11) | copy-start | bytes 196
  41.0 1.4 copy-start.9
  42.4 8.8 %copy-start.16 = (f32[16,3,9]{0,1,2:T(4,128)S(1)}, f32[16,3,9]{0,1,2:T(4,128)}, u32[]{:S(2)}) copy-start(f32[16,3,9]{0,1,2:T(4,128)} %param.12) | copy-start | bytes 5188
  42.6 16.5 %collective-permute-start.4 = (f32[16,64,32]{2,0,1:T(8,128)S(1)}, f32[16,64,32]{2,0,1:T(8,128)S(1)}, u32[]{:S(2)}, u32[]{:S(2)}) collective-permute-start(f32[16,64,32]{2,0,1:T(8,128)S(1)} %get-tuple-element.127), channel_id=1, source_target_pairs={{0,8},{8,16},{16,24},{24,32},{32,40},{40,48},{48,56},{56,64},{64,7... | collective-permute-start | bytes 393224 | tf_op jit(solution)/shard_map/ppermute | solution.py:15
  45.1 15.6 %collective-permute-start.5 = (f32[16,64,32]{2,0,1:T(8,128)S(1)}, f32[16,64,32]{2,0,1:T(8,128)S(1)}, u32[]{:S(2)}, u32[]{:S(2)}) collective-permute-start(f32[16,64,32]{2,0,1:T(8,128)S(1)} %get-tuple-element.128), channel_id=1, source_target_pairs={{8,0},{16,8},{24,16},{32,24},{40,32},{48,40},{56,48},{64,56},{72,6... | collective-permute-start | bytes 393224 | tf_op jit(solution)/shard_map/ppermute | solution.py:18
  59.1 13.0 %copy-start.7 = (f32[16,64,32]{2,0,1:T(8,128)}, f32[16,64,32]{2,0,1:T(8,128)S(1)}, u32[]{:S(2)}) copy-start(f32[16,64,32]{2,0,1:T(8,128)S(1)} %collective-permute-done.4) | copy-start | bytes 393220
  60.7 11.4 %copy-start.8 = (f32[16,64,32]{2,0,1:T(8,128)}, f32[16,64,32]{2,0,1:T(8,128)S(1)}, u32[]{:S(2)}) copy-start(f32[16,64,32]{2,0,1:T(8,128)S(1)} %collective-permute-done.5) | copy-start | bytes 393220
  60.7 5.9 %collective-permute-start.6 = (f32[16,1,192]{2,0,1:T(8,128)S(1)}, f32[16,1,192]{2,0,1:T(8,128)S(1)}, u32[]{:S(2)}, u32[]{:S(2)}) collective-permute-start(f32[16,1,192]{2,0,1:T(8,128)S(1)} %get-tuple-element.116), channel_id=1, source_target_pairs={{0,1},{1,2},{2,3},{3,4},{4,5},{5,6},{6,7},{8,9},{9,10},{10,11},{11... | collective-permute-start | bytes 36872 | tf_op jit(solution)/shard_map/ppermute | solution.py:15
  63.5 7.7 %collective-permute-start.7 = (f32[16,1,192]{2,0,1:T(8,128)S(1)}, f32[16,1,192]{2,0,1:T(8,128)S(1)}, u32[]{:S(2)}, u32[]{:S(2)}) collective-permute-start(f32[16,1,192]{2,0,1:T(8,128)S(1)} %get-tuple-element.117), channel_id=1, source_target_pairs={{1,0},{2,1},{3,2},{4,3},{5,4},{6,5},{7,6},{9,8},{10,9},{11,10},{12... | collective-permute-start | bytes 36872 | tf_op jit(solution)/shard_map/ppermute | solution.py:18
  72.1 4.5 %copy-start.17 = (f32[16,64,128]{2,1,0:T(8,128)S(1)}, f32[16,64,128]{2,1,0:T(8,128)}, u32[]{:S(2)}) copy-start(f32[16,64,128]{2,1,0:T(8,128)} %param.15) | copy-start | bytes 1572868
  72.1 4.5 %copy-start.20 = (f32[16]{0:T(128)S(1)}, f32[16]{0:T(128)}, u32[]{:S(2)}) copy-start(f32[16]{0:T(128)} %param.14) | copy-start | bytes 196
  76.7 1.8 copy-start.11
  78.5 3.0 %copy-start.14 = (f32[16,64,128]{2,0,1:T(8,128)}, f32[16,64,128]{2,0,1:T(8,128)S(1)}, u32[]{:S(2)}) copy-start(f32[16,64,128]{2,0,1:T(8,128)S(1)} %get-tuple-element.103) | copy-start | bytes 1572868
  81.5 9.9 %copy-start.3 = (f32[16,64,128]{2,0,1:T(8,128)}, f32[16,64,128]{2,0,1:T(8,128)S(1)}, u32[]{:S(2)}) copy-start(f32[16,64,128]{2,0,1:T(8,128)S(1)} %get-tuple-element.190) | copy-start | bytes 1572868
  82.7 15.8 %collective-permute-start.8 = (f32[16,64,32]{2,0,1:T(8,128)}, f32[16,64,32]{2,0,1:T(8,128)}, u32[]{:S(2)}, u32[]{:S(2)}) collective-permute-start(f32[16,64,32]{2,0,1:T(8,128)} %get-tuple-element.124), channel_id=1, source_target_pairs={{0,8},{8,16},{16,24},{24,32},{32,40},{40,48},{48,56},{56,64},{64,7... | collective-permute-start | bytes 393224 | tf_op jit(solution)/shard_map/ppermute | solution.py:15
  86.8 12.8 %collective-permute-start.9 = (f32[16,64,32]{2,0,1:T(8,128)}, f32[16,64,32]{2,0,1:T(8,128)}, u32[]{:S(2)}, u32[]{:S(2)}) collective-permute-start(f32[16,64,32]{2,0,1:T(8,128)} %get-tuple-element.125), channel_id=1, source_target_pairs={{8,0},{16,8},{24,16},{32,24},{40,32},{48,40},{56,48},{64,56},{72,6... | collective-permute-start | bytes 393224 | tf_op jit(solution)/shard_map/ppermute | solution.py:18
  96.4 3.2 %copy-start.4 = (f32[16,64,128]{2,0,1:T(8,128)S(1)}, f32[16,64,128]{2,0,1:T(8,128)}, u32[]{:S(2)}) copy-start(f32[16,64,128]{2,0,1:T(8,128)} %copy-done.3) | copy-start | bytes 1572868
  98.5 8.0 %copy-start.13 = (f32[16,64,128]{2,0,1:T(8,128)S(1)}, f32[16,64,128]{2,0,1:T(8,128)}, u32[]{:S(2)}) copy-start(f32[16,64,128]{2,0,1:T(8,128)} %get-tuple-element.126) | copy-start | bytes 1572868
  100.4 7.1 %collective-permute-start.10 = (f32[16,1,192]{2,0,1:T(8,128)S(1)}, f32[16,1,192]{2,0,1:T(8,128)S(1)}, u32[]{:S(2)}, u32[]{:S(2)}) collective-permute-start(f32[16,1,192]{2,0,1:T(8,128)S(1)} %get-tuple-element.112), channel_id=1, source_target_pairs={{0,1},{1,2},{2,3},{3,4},{4,5},{5,6},{6,7},{8,9},{9,10},{10,11},{11... | collective-permute-start | bytes 36872 | tf_op jit(solution)/shard_map/ppermute | solution.py:15
  104.6 7.7 %collective-permute-start.11 = (f32[16,1,192]{2,0,1:T(8,128)S(1)}, f32[16,1,192]{2,0,1:T(8,128)S(1)}, u32[]{:S(2)}, u32[]{:S(2)}) collective-permute-start(f32[16,1,192]{2,0,1:T(8,128)S(1)} %get-tuple-element.113), channel_id=1, source_target_pairs={{1,0},{2,1},{3,2},{4,3},{5,4},{6,5},{7,6},{9,8},{10,9},{11,10},{12... | collective-permute-start | bytes 36872 | tf_op jit(solution)/shard_map/ppermute | solution.py:18
  107.5 7.3 %copy-start.12 = (f32[16,64,128]{2,0,1:T(8,128)S(1)}, f32[16,64,128]{2,0,1:T(8,128)}, u32[]{:S(2)}) copy-start(f32[16,64,128]{2,0,1:T(8,128)} %get-tuple-element.188) | copy-start | bytes 1572868
  114.8 6.4 %copy-start.10 = (f32[16,64,128]{2,0,1:T(8,128)S(1)}, f32[16,64,128]{2,0,1:T(8,128)}, u32[]{:S(2)}) copy-start(f32[16,64,128]{2,0,1:T(8,128)} %copy-done.9) | copy-start | bytes 1572868
  125.0 9.7 %copy-start.2 = (f32[16,64,160]{2,0,1:T(8,128)S(1)}, f32[16,64,160]{2,0,1:T(8,128)}, u32[]{:S(2)}) copy-start(f32[16,64,160]{2,0,1:T(8,128)} %copy-done.1) | copy-start | bytes 1966084
  125.0 9.7 %copy-start.6 = (f32[16,64,32]{2,0,1:T(8,128)S(1)}, f32[16,64,32]{2,0,1:T(8,128)}, u32[]{:S(2)}) copy-start(f32[16,64,32]{2,0,1:T(8,128)} %copy-done.5) | copy-start | bytes 393220
  126.2 110.5 %collective-permute-start.12 = (f32[16,64,32]{2,0,1:T(8,128)}, f32[16,64,32]{2,0,1:T(8,128)S(1)}, u32[]{:S(2)}, u32[]{:S(2)}) collective-permute-start(f32[16,64,32]{2,0,1:T(8,128)} %get-tuple-element.122), channel_id=1, source_target_pairs={{0,8},{8,16},{16,24},{24,32},{32,40},{40,48},{48,56},{56,64},{64,7... | collective-permute-start | bytes 393224 | tf_op jit(solution)/shard_map/ppermute | solution.py:15
  129.9 106.8 %collective-permute-start.13 = (f32[16,64,32]{2,0,1:T(8,128)}, f32[16,64,32]{2,0,1:T(8,128)}, u32[]{:S(2)}, u32[]{:S(2)}) collective-permute-start(f32[16,64,32]{2,0,1:T(8,128)} %get-tuple-element.123), channel_id=1, source_target_pairs={{8,0},{16,8},{24,16},{32,24},{40,32},{48,40},{56,48},{64,56},{72,6... | collective-permute-start | bytes 393224 | tf_op jit(solution)/shard_map/ppermute | solution.py:18
  237.5 8.9 %collective-permute-start.14 = (f32[16,1,192]{2,0,1:T(8,128)S(1)}, f32[16,1,192]{2,0,1:T(8,128)S(1)}, u32[]{:S(2)}, u32[]{:S(2)}) collective-permute-start(f32[16,1,192]{2,0,1:T(8,128)S(1)} %get-tuple-element.108), channel_id=1, source_target_pairs={{0,1},{1,2},{2,3},{3,4},{4,5},{5,6},{6,7},{8,9},{9,10},{10,11},{11... | collective-permute-start | bytes 36872 | tf_op jit(solution)/shard_map/ppermute | solution.py:15
  242.4 7.7 %collective-permute-start.15 = (f32[16,1,192]{2,0,1:T(8,128)S(1)}, f32[16,1,192]{2,0,1:T(8,128)S(1)}, u32[]{:S(2)}, u32[]{:S(2)}) collective-permute-start(f32[16,1,192]{2,0,1:T(8,128)S(1)} %get-tuple-element.109), channel_id=1, source_target_pairs={{1,0},{2,1},{3,2},{4,3},{5,4},{6,5},{7,6},{9,8},{10,9},{11,10},{12... | collective-permute-start | bytes 36872 | tf_op jit(solution)/shard_map/ppermute | solution.py:18
where the time goes:
time: 260 us; the launch traced here: 259 us
  blocking collectives  98.3 us (38%)
  starting transfers between devices  62.9 us (24%)
  waiting for transfers between devices  39.3 us (15%)
  other arithmetic  37.6 us (14%)
  matrix products  12.1 us (5%)
  local copies, waits for them, and re-layouts  7.58 us (3%)
    psum x1, blocking collectives, per_device(): lax.psum((gkern_front, gmix_front, gbias_front, gkern_back, gmix_back, gb...  98.3 us
    ppermute x8, starting transfers between devices, with_halo(): lax.ppermute(lax.slice_in_dim(block, 0, width, axis=dim), axis, backward)  36 us
    ppermute x8, starting transfers between devices, with_halo(): lax.ppermute(lax.slice_in_dim(block, block.shape[dim] - width, None, axis...  26.9 us
    ppermute x8, waiting for transfers between devices, with_halo(): lax.ppermute(lax.slice_in_dim(block, 0, width, axis=dim), axis, backward)  21.9 us
    ppermute x8, waiting for transfers between devices, with_halo(): lax.ppermute(lax.slice_in_dim(block, block.shape[dim] - width, None, axis...  17.5 us
    add x3, other arithmetic, depthwise(): total_sum + kernel_weight[:, row_index, column_index][:, None, None] * pa...  14.2 us
    reduce_sum x2, other arithmetic, tap_grads(): jnp.sum(upward_gradient * padded_input[:, row_index:row_index + row_count...  7.79 us
    reduce_sum x1, other arithmetic, per_device(): gbias_front = jnp.sum(grad_front, axis=(1, 2))  6.43 us
  transfers between devices with their start and end apart: 16, of which 9 were waited for; matrix products, arithmetic and copies ran while one was open for 5% of the time, Pallas kernels for 0%

commit v1 on v0

--- a/solution.py
+++ b/solution.py
@@ -117,9 +117,9 @@
     signal_grad = depthwise(
         spread(under_front, kernel_extent, 1), kernel_front[:, ::-1, ::-1], row_count, column_count
     )
-    totals = lax.psum(
-        (gkern_front, gmix_front, gbias_front, gkern_back, gmix_back, gbias_back), ("tick", "wire")
-    )
+    totals = (gkern_front, gmix_front, gbias_front, gkern_back, gmix_back, gbias_back)
+    for mesh_axis in ("wire", "tick"):
+        totals = lax.psum(totals, mesh_axis)
     factor = 1.0 / math.sqrt(
         row_count * lax.axis_size("wire") * column_count * lax.axis_size("tick")
     )

time: 260 us -> 474 us (1.82)
  the two profiles are of different devices: /device:TPU:30 before, /device:TPU:38 now
where the time goes in v1:
time: 474 us; the launch traced here: 473 us
  blocking collectives  308 us (65%)
  starting transfers between devices  67.6 us (14%)
  waiting for transfers between devices  38.7 us (8%)
  other arithmetic  37.6 us (8%)
  matrix products  12.1 us (3%)
  local copies, waits for them, and re-layouts  7.58 us (2%)
    psum x2, blocking collectives, per_device(): totals = lax.psum(totals, mesh_axis)  308 us
    ppermute x8, starting transfers between devices, with_halo(): lax.ppermute(lax.slice_in_dim(block, 0, width, axis=dim), axis, backward)  44.2 us
    ppermute x8, starting transfers between devices, with_halo(): lax.ppermute(lax.slice_in_dim(block, block.shape[dim] - width, None, axis...  23.4 us
    ppermute x8, waiting for transfers between devices, with_halo(): lax.ppermute(lax.slice_in_dim(block, 0, width, axis=dim), axis, backward)  20.9 us
    ppermute x8, waiting for transfers between devices, with_halo(): lax.ppermute(lax.slice_in_dim(block, block.shape[dim] - width, None, axis...  17.7 us
    add x3, other arithmetic, depthwise(): total_sum + kernel_weight[:, row_index, column_index][:, None, None] * pa...  14.2 us
  transfers between devices with their start and end apart: 16, of which 8 were waited for; matrix products, arithmetic and copies ran while one was open for 3% of the time, Pallas kernels for 0%

profile of v1, /device:TPU:38, one launch (start us, length us, event | category | flops | bytes accessed | tf_op | source)
XLA Modules:
  0.0 473.1 jit_solution(9498058100045949811)
XLA Ops:
  0.6 0.0 copy-start
  0.6 1.4 constant_dynamic-update-slice_fusion.1
  2.0 0.0 copy-start.15
  2.0 0.2 fusion.104
  2.2 1.9 collective-permute-start
  4.1 10.3 %collective-permute-start.1 = (f32[16,64,32]{2,0,1:T(8,128)S(1)}, f32[16,64,32]{2,0,1:T(8,128)S(1)}, u32[]{:S(2)}, u32[]{:S(2)}) collective-permute-start(f32[16,64,32]{2,0,1:T(8,128)S(1)} %get-tuple-element.138), channel_id=1, source_target_pairs={{8,0},{16,8},{24,16},{32,24},{40,32},{48,40},{56,48},{64,56},{72,6... | collective-permute-start | bytes 393224 | tf_op jit(solution)/shard_map/ppermute | solution.py:18
  14.5 10.5 %collective-permute-done = f32[16,64,32]{2,0,1:T(8,128)S(1)} collective-permute-done((f32[16,64,32]{2,0,1:T(8,128)S(1)}, f32[16,64,32]{2,0,1:T(8,128)S(1)}, u32[]{:S(2)}, u32[]{:S(2)}) %collective-permute-start) | collective-permute-done | bytes 131104 | tf_op jit(solution)/shard_map/ppermute | solution.py:15
  25.0 0.1 pad_maximum_fusion.24
  25.0 3.0 collective-permute-start.2
  28.0 2.9 collective-permute-start.3
  30.9 0.1 constant_dynamic-update-slice_fusion
  31.0 4.8 %collective-permute-done.3 = f32[16,1,192]{2,0,1:T(8,128)S(1)} collective-permute-done((f32[16,1,192]{2,0,1:T(8,128)S(1)}, f32[16,1,192]{2,0,1:T(8,128)S(1)}, u32[]{:S(2)}, u32[]{:S(2)}) %collective-permute-start.3) | collective-permute-done | bytes 12320 | tf_op jit(solution)/shard_map/ppermute | solution.py:18
  35.8 0.9 maximum_maximum_fusion
  36.7 0.0 copy-start.18
  36.7 0.0 copy-start.19
  36.7 3.9 multiply_add_fusion.1
  40.7 1.4 fusion.93
  42.1 0.2 fusion.103
  42.3 2.7 collective-permute-start.4
  45.0 7.1 %collective-permute-start.5 = (f32[16,64,32]{2,0,1:T(8,128)S(1)}, f32[16,64,32]{2,0,1:T(8,128)S(1)}, u32[]{:S(2)}, u32[]{:S(2)}) collective-permute-start(f32[16,64,32]{2,0,1:T(8,128)S(1)} %get-tuple-element.134), channel_id=1, source_target_pairs={{8,0},{16,8},{24,16},{32,24},{40,32},{48,40},{56,48},{64,56},{72,6... | collective-permute-start | bytes 393224 | tf_op jit(solution)/shard_map/ppermute | solution.py:18
  52.1 7.2 %collective-permute-done.4 = f32[16,64,32]{2,0,1:T(8,128)S(1)} collective-permute-done((f32[16,64,32]{2,0,1:T(8,128)S(1)}, f32[16,64,32]{2,0,1:T(8,128)S(1)}, u32[]{:S(2)}, u32[]{:S(2)}) %collective-permute-start.4) | collective-permute-done | bytes 131104 | tf_op jit(solution)/shard_map/ppermute | solution.py:15
  59.4 2.3 collective-permute-done.5
  61.6 0.1 pad_maximum_fusion.21
  61.7 2.5 collective-permute-start.6
  64.3 3.3 collective-permute-start.7
  67.6 4.4 collective-permute-done.7
  72.0 0.9 maximum_maximum_fusion.1
  72.9 0.0 copy-start.17
  72.9 0.0 copy-start.20
  72.9 4.5 multiply_add_fusion
  77.5 1.8 fusion.98
  79.3 3.0 multiply_reduce_fusion.18
  82.3 1.1 fusion.102
  83.5 2.7 collective-permute-start.8
  86.1 7.3 %collective-permute-start.9 = (f32[16,64,32]{2,0,1:T(8,128)}, f32[16,64,32]{2,0,1:T(8,128)}, u32[]{:S(2)}, u32[]{:S(2)}) collective-permute-start(f32[16,64,32]{2,0,1:T(8,128)} %get-tuple-element.131), channel_id=1, source_target_pairs={{8,0},{16,8},{24,16},{32,24},{40,32},{48,40},{56,48},{64,56},{72,6... | collective-permute-start | bytes 393224 | tf_op jit(solution)/shard_map/ppermute | solution.py:18
  93.5 4.9 %multiply_reduce_fusion.9 = (f32[16]{0:T(128)S(1)}, f32[16]{0:T(128)S(1)}, f32[16]{0:T(128)S(1)}, f32[16]{0:T(128)S(1)}, f32[16]{0:T(128)S(1)}, /*index=5*/f32[1...) fusion(f32[16,64,128]{2,0,1:T(8,128)} %copy-done.3, f32[16,64,32]{2,0,1:T(8,128)} %copy-done.8, ...), kind=kLoop, calls=%fused_computation.201 | loop fusion | flops 3932016 | bytes 1835584 | tf_op jit(solution)/shard_map/reduce_sum | solution.py:52
  98.5 2.0 convolution_bitcast_fusion.2
  100.5 2.3 collective-permute-done.9
  102.8 0.8 pad_maximum_fusion.18
  103.6 2.4 collective-permute-start.10
  106.1 3.4 collective-permute-start.11
  109.5 1.0 copy.26
  110.5 3.4 collective-permute-done.11
  113.8 2.4 maximum_maximum_fusion.2
  116.3 6.4 %fusion.99 = (f32[16]{0:T(128)S(1)}, f32[16,64,128]{2,0,1:T(8,128)S(1)}) fusion(f32[16,64,128]{2,0,1:T(8,128)S(1)} %copy-done.12, f32[16,65,192]{2,0,1:T(8,128)S(1)} %get-tuple-element.117, f32[16]{0:T(128)S(1)} %get-tuple-element.139, f32[16]{0:T(128)S(1)} %get-tuple-element.158, f32[16]{0:T(128)S(1)} %get-tuple-element.163, f32[16]{0:T(128)S(1)} %get-tuple-element.162, ...), kind=kLoop, calls=%fused_computation.333 | loop fusion | flops 9175024 | bytes 11273984 | tf_op jit(solution)/shard_map/reduce_sum | solution.py:112
  122.7 0.8 convolution_bitcast_fusion.3
  123.5 3.0 multiply_reduce_fusion.45
  126.6 1.1 fusion.101
  127.7 1.9 collective-permute-start.12
  129.6 7.9 %collective-permute-start.13 = (f32[16,64,32]{2,0,1:T(8,128)}, f32[16,64,32]{2,0,1:T(8,128)}, u32[]{:S(2)}, u32[]{:S(2)}) collective-permute-start(f32[16,64,32]{2,0,1:T(8,128)} %get-tuple-element.129), channel_id=1, source_target_pairs={{8,0},{16,8},{24,16},{32,24},{40,32},{48,40},{56,48},{64,56},{72,6... | collective-permute-start | bytes 393224 | tf_op jit(solution)/shard_map/ppermute | solution.py:18
  137.5 2.9 multiply_reduce_fusion.36
  140.5 33.3 %all-reduce.1 = (f32[16,3,9]{0,2,1:T(8,128)S(1)}, f32[16,16]{1,0:T(8,128)S(1)}, f32[16]{0:T(128)S(1)}, f32[16,3,9]{0,2,1:T(8,128)S(1)}, f32[16,16]{1,0:T(8,128)S(1)}, /*index=5*/f32[16]{0:T(128)S(1)}) all-reduce(f32[16,3,9]{0,2,1:T(8,128)S(1)} %pad_maximum_fusion.11, ...), channel_id=1, replica_groups=mesh['tick'=64,'wire'=8] {'wire'}, use_global_device_ids=true, to_apply=%region_27.28 | all-reduce | flops 1408 | bytes 11264 | tf_op jit(solution)/shard_map/psum | solution.py:122
  173.8 275.0 %all-reduce = (f32[16,3,9]{0,2,1:T(8,128)S(1)}, f32[16,16]{1,0:T(8,128)S(1)}, f32[16]{0:T(128)S(1)}, f32[16,3,9]{0,2,1:T(8,128)S(1)}, f32[16,16]{1,0:T(8,128)S(1)}, /*index=5*/f32[16]{0:T(128)S(1)}) all-reduce(f32[16,3,9]{0,2,1:T(8,128)S(1)} %get-tuple-element.102, ...), channel_id=1, replica_groups=mesh['tick'=64,'wire'=8] {'tick'}, use_global_device_ids=true, to_apply=%region_28.29 | all-reduce | flops 1408 | bytes 11264 | tf_op jit(solution)/shard_map/psum | solution.py:122
  448.9 0.6 broadcast_multiply_fusion.2
  449.5 0.8 pad_maximum_fusion.15
  450.3 6.3 %collective-permute-start.14 = (f32[16,1,192]{2,0,1:T(8,128)S(1)}, f32[16,1,192]{2,0,1:T(8,128)S(1)}, u32[]{:S(2)}, u32[]{:S(2)}) collective-permute-start(f32[16,1,192]{2,0,1:T(8,128)S(1)} %get-tuple-element.114), channel_id=1, source_target_pairs={{0,1},{1,2},{2,3},{3,4},{4,5},{5,6},{6,7},{8,9},{9,10},{10,11},{11... | collective-permute-start | bytes 36872 | tf_op jit(solution)/shard_map/ppermute | solution.py:15
  456.6 2.1 collective-permute-start.15
  458.7 0.5 broadcast_multiply_fusion.4
  459.2 0.6 copy.28
  459.9 0.6 copy.29
  460.5 3.8 collective-permute-done.15
  464.3 2.1 maximum_maximum_fusion.3
  466.4 5.7 %fusion.14 = f32[16,64,128]{2,0,1:T(8,128)S(1)} fusion(f32[16,64,128]{2,0,1:T(8,128)S(1)} %get-tuple-element.195, f32[16,64,32]{2,0,1:T(8,128)} %collective-permute-done.13, f32[16,64,32]{2,0,1:T(8,128)S(1)} %collective-permute-done.12, f32[16,65,192]{2,0,1:T(8,128)S(1)} %get-tuple-element.113, f32[16,65,192]{2,0,1:T(8,128)S(1)} %get-tuple-element.112, ...), kind=kLoop, calls=%fused_computation.70 | loop fusion | flops 7995392 | bytes 10749632 | tf_op jit(solution)/shard_map/add | solution.py:33
  472.2 1.0 copy.27
  (57 shorter events, 0.4 us)
Async XLA Ops:
  0.6 76.8 %copy-start = (f32[16,16]{1,0:T(8,128)S(1)}, f32[16,16]{1,0:T(8,128)}, u32[]{:S(2)}) copy-start(f32[16,16]{1,0:T(8,128)} %param.13) | copy-start | bytes 3076
  2.0 12.4 %copy-start.15 = (f32[16,3,9]{0,1,2:T(4,128)S(1)}, f32[16,3,9]{0,1,2:T(4,128)}, u32[]{:S(2)}) copy-start(f32[16,3,9]{0,1,2:T(4,128)} %param.9) | copy-start | bytes 5188
  2.2 22.7 %collective-permute-start = (f32[16,64,32]{2,0,1:T(8,128)S(1)}, f32[16,64,32]{2,0,1:T(8,128)S(1)}, u32[]{:S(2)}, u32[]{:S(2)}) collective-permute-start(f32[16,64,32]{2,0,1:T(8,128)S(1)} %get-tuple-element.137), channel_id=1, source_target_pairs={{0,8},{8,16},{16,24},{24,32},{32,40},{40,48},{48,56},{56,64},{64,7... | collective-permute-start | bytes 393224 | tf_op jit(solution)/shard_map/ppermute | solution.py:15
  4.1 20.8 %collective-permute-start.1 = (f32[16,64,32]{2,0,1:T(8,128)S(1)}, f32[16,64,32]{2,0,1:T(8,128)S(1)}, u32[]{:S(2)}, u32[]{:S(2)}) collective-permute-start(f32[16,64,32]{2,0,1:T(8,128)S(1)} %get-tuple-element.138), channel_id=1, source_target_pairs={{8,0},{16,8},{24,16},{32,24},{40,32},{48,40},{56,48},{64,56},{72,6... | collective-permute-start | bytes 393224 | tf_op jit(solution)/shard_map/ppermute | solution.py:18
  25.0 11.7 %copy-start.5 = (f32[16,64,32]{2,0,1:T(8,128)}, f32[16,64,32]{2,0,1:T(8,128)S(1)}, u32[]{:S(2)}) copy-start(f32[16,64,32]{2,0,1:T(8,128)S(1)} %collective-permute-done) | copy-start | bytes 393220
  25.0 5.9 %collective-permute-start.2 = (f32[16,1,192]{2,0,1:T(8,128)S(1)}, f32[16,1,192]{2,0,1:T(8,128)S(1)}, u32[]{:S(2)}, u32[]{:S(2)}) collective-permute-start(f32[16,1,192]{2,0,1:T(8,128)S(1)} %get-tuple-element.126), channel_id=1, source_target_pairs={{0,1},{1,2},{2,3},{3,4},{4,5},{5,6},{6,7},{8,9},{9,10},{10,11},{11... | collective-permute-start | bytes 36872 | tf_op jit(solution)/shard_map/ppermute | solution.py:15
  28.0 7.7 %collective-permute-start.3 = (f32[16,1,192]{2,0,1:T(8,128)S(1)}, f32[16,1,192]{2,0,1:T(8,128)S(1)}, u32[]{:S(2)}, u32[]{:S(2)}) collective-permute-start(f32[16,1,192]{2,0,1:T(8,128)S(1)} %get-tuple-element.127), channel_id=1, source_target_pairs={{1,0},{2,1},{3,2},{4,3},{5,4},{6,5},{7,6},{9,8},{10,9},{11,10},{12... | collective-permute-start | bytes 36872 | tf_op jit(solution)/shard_map/ppermute | solution.py:18
  31.0 5.7 %copy-start.1 = (f32[16,64,160]{2,0,1:T(8,128)}, f32[16,64,160]{2,0,1:T(8,128)S(1)}, u32[]{:S(2)}) copy-start(f32[16,64,160]{2,0,1:T(8,128)S(1)} %constant_dynamic-update-slice_fusion) | copy-start | bytes 1966084
  36.7 4.0 copy-start.18
  36.7 4.0 copy-start.19
  40.7 1.4 copy-start.9
  42.1 10.0 %copy-start.16 = (f32[16,3,9]{0,1,2:T(4,128)S(1)}, f32[16,3,9]{0,1,2:T(4,128)}, u32[]{:S(2)}) copy-start(f32[16,3,9]{0,1,2:T(4,128)} %param.12) | copy-start | bytes 5188
  42.3 17.1 %collective-permute-start.4 = (f32[16,64,32]{2,0,1:T(8,128)S(1)}, f32[16,64,32]{2,0,1:T(8,128)S(1)}, u32[]{:S(2)}, u32[]{:S(2)}) collective-permute-start(f32[16,64,32]{2,0,1:T(8,128)S(1)} %get-tuple-element.133), channel_id=1, source_target_pairs={{0,8},{8,16},{16,24},{24,32},{32,40},{40,48},{48,56},{56,64},{64,7... | collective-permute-start | bytes 393224 | tf_op jit(solution)/shard_map/ppermute | solution.py:15
  45.0 16.7 %collective-permute-start.5 = (f32[16,64,32]{2,0,1:T(8,128)S(1)}, f32[16,64,32]{2,0,1:T(8,128)S(1)}, u32[]{:S(2)}, u32[]{:S(2)}) collective-permute-start(f32[16,64,32]{2,0,1:T(8,128)S(1)} %get-tuple-element.134), channel_id=1, source_target_pairs={{8,0},{16,8},{24,16},{32,24},{40,32},{48,40},{56,48},{64,56},{72,6... | collective-permute-start | bytes 393224 | tf_op jit(solution)/shard_map/ppermute | solution.py:18
  59.4 13.5 %copy-start.7 = (f32[16,64,32]{2,0,1:T(8,128)}, f32[16,64,32]{2,0,1:T(8,128)S(1)}, u32[]{:S(2)}) copy-start(f32[16,64,32]{2,0,1:T(8,128)S(1)} %collective-permute-done.4) | copy-start | bytes 393220
  61.6 11.3 %copy-start.8 = (f32[16,64,32]{2,0,1:T(8,128)}, f32[16,64,32]{2,0,1:T(8,128)S(1)}, u32[]{:S(2)}) copy-start(f32[16,64,32]{2,0,1:T(8,128)S(1)} %collective-permute-done.5) | copy-start | bytes 393220
  61.7 5.9 %collective-permute-start.6 = (f32[16,1,192]{2,0,1:T(8,128)S(1)}, f32[16,1,192]{2,0,1:T(8,128)S(1)}, u32[]{:S(2)}, u32[]{:S(2)}) collective-permute-start(f32[16,1,192]{2,0,1:T(8,128)S(1)} %get-tuple-element.122), channel_id=1, source_target_pairs={{0,1},{1,2},{2,3},{3,4},{4,5},{5,6},{6,7},{8,9},{9,10},{10,11},{11... | collective-permute-start | bytes 36872 | tf_op jit(solution)/shard_map/ppermute | solution.py:15
  64.3 7.7 %collective-permute-start.7 = (f32[16,1,192]{2,0,1:T(8,128)S(1)}, f32[16,1,192]{2,0,1:T(8,128)S(1)}, u32[]{:S(2)}, u32[]{:S(2)}) collective-permute-start(f32[16,1,192]{2,0,1:T(8,128)S(1)} %get-tuple-element.123), channel_id=1, source_target_pairs={{1,0},{2,1},{3,2},{4,3},{5,4},{6,5},{7,6},{9,8},{10,9},{11,10},{12... | collective-permute-start | bytes 36872 | tf_op jit(solution)/shard_map/ppermute | solution.py:18
  72.9 4.5 copy-start.17
  72.9 4.5 copy-start.20
  77.4 1.8 copy-start.11
  79.3 3.0 copy-start.14
  82.3 11.1 %copy-start.3 = (f32[16,64,128]{2,0,1:T(8,128)}, f32[16,64,128]{2,0,1:T(8,128)S(1)}, u32[]{:S(2)}) copy-start(f32[16,64,128]{2,0,1:T(8,128)S(1)} %get-tuple-element.196) | copy-start | bytes 1572868
  83.5 17.0 %collective-permute-start.8 = (f32[16,64,32]{2,0,1:T(8,128)}, f32[16,64,32]{2,0,1:T(8,128)}, u32[]{:S(2)}, u32[]{:S(2)}) collective-permute-start(f32[16,64,32]{2,0,1:T(8,128)} %get-tuple-element.130), channel_id=1, source_target_pairs={{0,8},{8,16},{16,24},{24,32},{32,40},{40,48},{48,56},{56,64},{64,7... | collective-permute-start | bytes 393224 | tf_op jit(solution)/shard_map/ppermute | solution.py:15
  86.1 16.6 %collective-permute-start.9 = (f32[16,64,32]{2,0,1:T(8,128)}, f32[16,64,32]{2,0,1:T(8,128)}, u32[]{:S(2)}, u32[]{:S(2)}) collective-permute-start(f32[16,64,32]{2,0,1:T(8,128)} %get-tuple-element.131), channel_id=1, source_target_pairs={{8,0},{16,8},{24,16},{32,24},{40,32},{48,40},{56,48},{64,56},{72,6... | collective-permute-start | bytes 393224 | tf_op jit(solution)/shard_map/ppermute | solution.py:18
  98.4 4.4 copy-start.4
  100.5 9.0 %copy-start.13 = (f32[16,64,128]{2,0,1:T(8,128)S(1)}, f32[16,64,128]{2,0,1:T(8,128)}, u32[]{:S(2)}) copy-start(f32[16,64,128]{2,0,1:T(8,128)} %get-tuple-element.132) | copy-start | bytes 1572868
  103.6 6.8 %collective-permute-start.10 = (f32[16,1,192]{2,0,1:T(8,128)S(1)}, f32[16,1,192]{2,0,1:T(8,128)S(1)}, u32[]{:S(2)}, u32[]{:S(2)}) collective-permute-start(f32[16,1,192]{2,0,1:T(8,128)S(1)} %get-tuple-element.118), channel_id=1, source_target_pairs={{0,1},{1,2},{2,3},{3,4},{4,5},{5,6},{6,7},{8,9},{9,10},{10,11},{11... | collective-permute-start | bytes 36872 | tf_op jit(solution)/shard_map/ppermute | solution.py:15
  106.1 7.7 %collective-permute-start.11 = (f32[16,1,192]{2,0,1:T(8,128)S(1)}, f32[16,1,192]{2,0,1:T(8,128)S(1)}, u32[]{:S(2)}, u32[]{:S(2)}) collective-permute-start(f32[16,1,192]{2,0,1:T(8,128)S(1)} %get-tuple-element.119), channel_id=1, source_target_pairs={{1,0},{2,1},{3,2},{4,3},{5,4},{6,5},{7,6},{9,8},{10,9},{11,10},{12... | collective-permute-start | bytes 36872 | tf_op jit(solution)/shard_map/ppermute | solution.py:18
  110.5 5.8 %copy-start.12 = (f32[16,64,128]{2,0,1:T(8,128)S(1)}, f32[16,64,128]{2,0,1:T(8,128)}, u32[]{:S(2)}) copy-start(f32[16,64,128]{2,0,1:T(8,128)} %get-tuple-element.194) | copy-start | bytes 1572868
  116.3 6.4 %copy-start.10 = (f32[16,64,128]{2,0,1:T(8,128)S(1)}, f32[16,64,128]{2,0,1:T(8,128)}, u32[]{:S(2)}) copy-start(f32[16,64,128]{2,0,1:T(8,128)} %copy-done.9) | copy-start | bytes 1572868
  126.5 11.0 %copy-start.2 = (f32[16,64,160]{2,0,1:T(8,128)S(1)}, f32[16,64,160]{2,0,1:T(8,128)}, u32[]{:S(2)}) copy-start(f32[16,64,160]{2,0,1:T(8,128)} %copy-done.1) | copy-start | bytes 1966084
  126.5 11.0 %copy-start.6 = (f32[16,64,32]{2,0,1:T(8,128)S(1)}, f32[16,64,32]{2,0,1:T(8,128)}, u32[]{:S(2)}) copy-start(f32[16,64,32]{2,0,1:T(8,128)} %copy-done.5) | copy-start | bytes 393220
  127.7 321.8 %collective-permute-start.12 = (f32[16,64,32]{2,0,1:T(8,128)}, f32[16,64,32]{2,0,1:T(8,128)S(1)}, u32[]{:S(2)}, u32[]{:S(2)}) collective-permute-start(f32[16,64,32]{2,0,1:T(8,128)} %get-tuple-element.128), channel_id=1, source_target_pairs={{0,8},{8,16},{16,24},{24,32},{32,40},{40,48},{48,56},{56,64},{64,7... | collective-permute-start | bytes 393224 | tf_op jit(solution)/shard_map/ppermute | solution.py:15
  129.6 319.9 %collective-permute-start.13 = (f32[16,64,32]{2,0,1:T(8,128)}, f32[16,64,32]{2,0,1:T(8,128)}, u32[]{:S(2)}, u32[]{:S(2)}) collective-permute-start(f32[16,64,32]{2,0,1:T(8,128)} %get-tuple-element.129), channel_id=1, source_target_pairs={{8,0},{16,8},{24,16},{32,24},{40,32},{48,40},{56,48},{64,56},{72,6... | collective-permute-start | bytes 393224 | tf_op jit(solution)/shard_map/ppermute | solution.py:18
  450.3 10.2 %collective-permute-start.14 = (f32[16,1,192]{2,0,1:T(8,128)S(1)}, f32[16,1,192]{2,0,1:T(8,128)S(1)}, u32[]{:S(2)}, u32[]{:S(2)}) collective-permute-start(f32[16,1,192]{2,0,1:T(8,128)S(1)} %get-tuple-element.114), channel_id=1, source_target_pairs={{0,1},{1,2},{2,3},{3,4},{4,5},{5,6},{6,7},{8,9},{9,10},{10,11},{11... | collective-permute-start | bytes 36872 | tf_op jit(solution)/shard_map/ppermute | solution.py:15
  456.6 7.7 %collective-permute-start.15 = (f32[16,1,192]{2,0,1:T(8,128)S(1)}, f32[16,1,192]{2,0,1:T(8,128)S(1)}, u32[]{:S(2)}, u32[]{:S(2)}) collective-permute-start(f32[16,1,192]{2,0,1:T(8,128)S(1)} %get-tuple-element.115), channel_id=1, source_target_pairs={{1,0},{2,1},{3,2},{4,3},{5,4},{6,5},{7,6},{9,8},{10,9},{11,10},{12... | collective-permute-start | bytes 36872 | tf_op jit(solution)/shard_map/ppermute | solution.py:18
